TPU v7x, 32 devices: a whole 2x2x4 slice. The times are simulated.
32 devices in a mesh: seq: 16 (over z, x, core), head: 2 (over y).
Axes of the slice: x: 2, y: 2, z: 4, core: 2. Of those that a mesh axis runs over, the one named last changes fastest.
Arguments:
- queries: bfloat16 [4096, 4096], P('seq', 'head'), may hold values from -8 to 8
- keys: bfloat16 [4096, 4096], P('seq', 'head'), may hold values from -8 to 8
- values: bfloat16 [4096, 4096], P('seq', 'head'), may hold values from -6 to 6
- features: float32 [32, 128, 256], P('head'), may hold values from -6 to 6
- output_proj_weight: bfloat16 [4096, 4096], P('head', 'seq'), may hold values from -0.125 to 0.125
Outputs:
- mixed: bfloat16 [4096, 4096], P('seq', 'head')
All inputs are finite; a program needn't handle non-finite values.
Results may differ from a plain program's by a relative error of at most 0.005.
Values may be sent and summed in bfloat16 or wider, within the bound.
A program may use at most 192 MiB of HBM per device.

v0:
```python
import math
import jax
import jax.numpy as jnp
from jax import lax
from jax.sharding import PartitionSpec as P

DH = 128
M = 256
HIGH = lax.Precision.HIGHEST


def feature_map(x, direction):
    x = x * DH ** (-0.25)
    proj = jnp.einsum("htd,hdm->htm", x, direction, precision=HIGH)
    return jnp.exp(proj - 0.5 * jnp.sum(x * x, axis=-1, keepdims=True)) / math.sqrt(M)


def shards(queries, keys, values, features, output_proj_weight):
    tok_rows = queries.shape[0]
    local_heads = features.shape[0]
    devices, here = (lax.axis_size("seq"), lax.axis_index("seq"))
    halves, half = (lax.axis_size("head"), lax.axis_index("head"))

    def split_heads(arr):
        return arr.astype(jnp.float32).reshape(tok_rows, local_heads, DH).transpose(1, 0, 2)

    kf = feature_map(split_heads(keys), features)
    v = split_heads(values)
    v = jnp.concatenate([v, jnp.ones((local_heads, tok_rows, 8), jnp.float32)], axis=2)
    state = jnp.einsum("htp,htk->hpk", v, kf, precision=HIGH)
    states = lax.all_gather(state.astype(jnp.bfloat16), "seq")
    state, weight = lax.optimization_barrier((state, output_proj_weight))
    whole = lax.all_gather(weight, "seq", axis=1, tiled=True)
    qf = feature_map(split_heads(queries), features)
    lower = jnp.tril(jnp.ones((tok_rows, tok_rows), jnp.float32))
    scores = jnp.einsum("htm,hsm->hts", qf, kf, precision=HIGH) * lower
    both = jnp.einsum("hts,hsd->htd", scores, v, precision=HIGH)
    earlier = (jnp.arange(devices) < here)[:, None, None, None]
    prior = jnp.sum(jnp.where(earlier, states.astype(jnp.float32), 0.0), axis=0)
    both = both + jnp.einsum("htk,hpk->htp", qf, prior, precision=HIGH)
    attended = both[:, :, :DH] / both[:, :, DH : DH + 1]
    attended = attended.transpose(1, 0, 2).reshape(tok_rows, local_heads * DH).astype(jnp.bfloat16)
    partial = jnp.dot(attended, whole, preferred_element_type=jnp.float32)
    width = partial.shape[1] // halves
    total = lax.dynamic_slice_in_dim(partial, half * width, width, 1)
    for shift in range(1, halves):
        theirs = lax.rem(half + shift, halves)
        piece = lax.dynamic_slice_in_dim(partial, theirs * width, width, 1).astype(jnp.bfloat16)
        got = lax.ppermute(piece, "head", [(i, (i + shift) % halves) for i in range(halves)])
        total = total + got.astype(jnp.float32)
    return total.astype(jnp.bfloat16)


def solution(mesh):
    in_specs = (
        P("seq", "head"),
        P("seq", "head"),
        P("seq", "head"),
        P("head", None, None),
        P("head", "seq"),
    )
    return jax.shard_map(
        shards, mesh=mesh, in_specs=in_specs, out_specs=P("seq", "head"), check_vma=False
    )
```

profile of v0, /device:TPU:0, one launch (start us, length us, event | category | flops | bytes accessed | tf_op | source)
XLA Modules:
  0.0 298.5 jit_solution(12855215793351295603)
XLA Ops:
  6.5 0.0 copy-start
  6.5 0.0 all-gather.6.cloned.1.call-start
  6.5 2.0 fusion.8
  8.5 0.0 copy-done
  8.5 7.0 %fusion.7 = f32[16,256,256]{2,1,0:T(8,128)} fusion(f32[16,128,256]{2,1,0:T(8,128)S(1)} %copy-done, bf16[256,2048]{1,0:T(8,128)(2,1)} %param.6), kind=kOutput, calls=%fused_computation.11 | convolution fusion | flops 1611661312 | bytes 7340032 | tf_op jit(solution)/shard_map/htd,hdm->htm/dot_general | solution.py:14
  15.5 1.5 copy.11
  17.0 5.6 %fusion.5 = bf16[16,136,256]{2,1,0:T(8,128)(2,1)} fusion(f32[16,256,256]{2,1,0:T(8,128)} %fusion.7, f32[16,256]{1,0:T(8,128)S(1)} %broadcast_multiply_fusion, bf16[16,256,128]{1,2,0:T(8,128)(2,1)S(1)} %bitcast.55), kind=kOutput, calls=%fused_computation.8 | convolution fusion | flops 1713373184 | bytes 6373376 | tf_op jit(solution)/shard_map/htp,htk->hpk/dot_general | solution.py:30
  22.6 0.0 all-gather.6.cloned.1.call-update
  22.6 0.0 all-gather.4.cloned.1.call-start
  22.6 0.7 all-gather.4.cloned.1.call-update
  23.4 0.0 copy-start.2
  23.4 2.0 fusion.11
  25.4 4.9 %fusion.10 = f32[16,256,256]{2,1,0:T(8,128)S(1)} fusion(f32[16,128,256]{2,1,0:T(8,128)S(1)} %copy-done, bf16[256,2048]{1,0:T(8,128)(2,1)} %param.5), kind=kOutput, calls=%fused_computation.15 | convolution fusion | flops 1611661312 | bytes 7340032 | tf_op jit(solution)/shard_map/htd,hdm->htm/dot_general | solution.py:14
  30.3 0.0 copy-start.3
  30.3 2.0 copy-done.3
  32.3 0.0 copy-done.2
  32.3 7.0 %fusion.4 = f32[16,256,256]{2,1,0:T(8,128)} fusion(f32[16,256,256]{2,1,0:T(8,128)S(1)} %fusion.10, f32[16,256,256]{2,1,0:T(8,128)S(1)} %copy-done.2, f32[16,256]{1,0:T(8,128)S(1)} %broadcast_multiply_fusion, f32[16,256]{1,0:T(8,128)S(1)} %broadcast_multiply_fusion.1), kind=kOutput, calls=%fused_computation.7 | convolution fusion | flops 3225419776 | bytes 12615680 | tf_op jit(solution)/shard_map/htm,hsm->hts/dot_general | solution.py:36
  39.3 80.2 %all-gather.6.cloned.1.call-done = bf16[256,136,256]{2,1,0:T(8,128)(2,1)} async-done(((bf16[16,136,256]{2,1,0:T(8,128)(2,1)}), bf16[256,136,256]{2,1,0:T(8,128)(2,1)}) %all-gather.6.cloned.1.call-update) | async-done | bytes 17825808 | tf_op jit(solution)/shard_map/all_gather | solution.py:31
  119.5 0.0 copy-start.4
  119.5 11.7 %fusion = f32[16,136,256]{2,1,0:T(8,128)S(1)} fusion(bf16[16,16,136,256]{3,2,1,0:T(8,128)(2,1)} %bitcast.54, pred[16]{0:T(512)(128)(4,1)S(1)} %iota_compare_fusion.1), kind=kLoop, calls=%fused_computation.1 | loop fusion | flops 26181632 | bytes 20054032 | tf_op jit(solution)/shard_map/reduce_sum | solution.py:39
  131.2 0.0 copy-done.4
  131.2 0.0 copy-start.5
  131.2 5.5 %fusion.3 = f32[16,256,136]{1,2,0:T(8,128)S(1)} fusion(f32[16,136,256]{2,1,0:T(8,128)S(1)} %fusion, f32[16,256,256]{2,1,0:T(8,128)S(1)} %copy-done.4, f32[16,256]{1,0:T(8,128)S(1)} %broadcast_multiply_fusion.1), kind=kOutput, calls=%fused_computation.6 | convolution fusion | flops 1713373184 | bytes 8667136 | tf_op jit(solution)/shard_map/htk,hpk->htp/dot_general | solution.py:40
  136.6 0.0 copy-done.5
  136.6 2.7 fusion.23
  139.4 0.2 fusion.12
  139.7 112.3 %all-gather.4.cloned.1.call-done = bf16[2048,4096]{1,0:T(8,128)(2,1)} async-done(((bf16[2048,256]{1,0:T(8,128)(2,1)}), bf16[2048,4096]{1,0:T(8,128)(2,1)}) %all-gather.4.cloned.1.call-update) | async-done | bytes 16777232 | tf_op jit(solution)/shard_map/all_gather | solution.py:33
  252.0 0.0 copy-start.1
  252.0 8.3 %fusion.34 = f32[256,4096]{1,0:T(8,128)S(1)} fusion(bf16[256,2048]{0,1:T(8,128)(2,1)S(1)} %bitcast.57, bf16[2048,4096]{1,0:T(8,128)(2,1)} %all-gather.4.cloned.1.call-done), kind=kOutput, calls=%fused_computation.47 | convolution fusion | flops 4294967296 | bytes 22020096 | tf_op jit(solution)/shard_map/dot_general | solution.py:43
  260.3 0.0 copy-start.6
  260.3 1.9 copy-done.6
  262.2 1.1 dynamic-slice_convert_fusion
  263.3 1.5 collective-permute-start
  264.8 24.1 %collective-permute-done = bf16[256,2048]{1,0:T(8,128)(2,1)S(1)} collective-permute-done((bf16[256,2048]{1,0:T(8,128)(2,1)}, bf16[256,2048]{1,0:T(8,128)(2,1)S(1)}, u32[]{:S(2)}, u32[]{:S(2)}) %collective-permute-start) | collective-permute-done | bytes 1048608 | tf_op jit(solution)/shard_map/ppermute | solution.py:49
  288.9 2.9 add_convert_fusion
  291.7 0.0 copy-done.1
  (6 shorter events, 0.0 us)
Async XLA Ops:
  6.5 2.0 copy-start
  6.5 112.9 %all-gather.6.cloned.1.call-start = ((), (), s32[]{:S(2)}) async-start(), calls=%async_computation.1 | async-start | bytes 18939904 | tf_op jit(solution)/shard_map/all_gather | solution.py:31
  22.6 229.4 %all-gather.4.cloned.1.call-start = ((), (), s32[]{:S(2)}) async-start(), calls=%async_computation | async-start | bytes 17825792 | tf_op jit(solution)/shard_map/all_gather | solution.py:33
  23.4 9.0 %copy-start.2 = (f32[16,256,256]{2,1,0:T(8,128)S(1)}, f32[16,256,256]{2,1,0:T(8,128)}, u32[]{:S(2)}) copy-start(f32[16,256,256]{2,1,0:T(8,128)} %fusion.7) | copy-start | bytes 12582916
  30.3 2.0 copy-start.3
  119.5 11.7 %copy-start.4 = (f32[16,256,256]{2,1,0:T(8,128)S(1)}, f32[16,256,256]{2,1,0:T(8,128)}, u32[]{:S(2)}) copy-start(f32[16,256,256]{2,1,0:T(8,128)} %copy-done.3) | copy-start | bytes 12582916
  131.2 5.5 %copy-start.5 = (f32[16,256,256]{2,1,0:T(8,128)S(1)}, f32[16,256,256]{2,1,0:T(8,128)}, u32[]{:S(2)}) copy-start(f32[16,256,256]{2,1,0:T(8,128)} %fusion.4) | copy-start | bytes 12582916
  252.0 39.7 %copy-start.1 = (f32[16,128,256]{2,1,0:T(8,128)S(1)}, f32[16,128,256]{2,1,0:T(8,128)}, u32[]{:S(2)}) copy-start(f32[16,128,256]{2,1,0:T(8,128)} %param.8) | copy-start | bytes 6291460
  260.3 1.9 copy-start.6
  263.3 25.5 %collective-permute-start = (bf16[256,2048]{1,0:T(8,128)(2,1)}, bf16[256,2048]{1,0:T(8,128)(2,1)S(1)}, u32[]{:S(2)}, u32[]{:S(2)}) collective-permute-start(bf16[256,2048]{1,0:T(8,128)(2,1)} %dynamic-slice_convert_fusion), channel_id=1, source_target_pairs={{0,1},{1,0},{2,3},{3,2},{4,5},{5,4},{6,7},{7,6},{8,9},{9,8},{10,11... | collective-permute-start | bytes 3145736 | tf_op jit(solution)/shard_map/ppermute | solution.py:49
Sparse Core Ops, SparseCore 0:
  22.7 96.7 all-gather.5
  121.6 130.3 all-gather.3
where the time goes:
time: 299 us
  waiting for transfers between devices  217 us (73%)
  matrix products  40.9 us (14%)
  other arithmetic  18.8 us (6%)
  between operations  13.6 us (5%)
  local copies, waits for them, and re-layouts  6.56 us (2%)
    all_gather x1, waiting for transfers between devices, shards(): whole = lax.all_gather(weight, 'seq', axis=1, tiled=True)  112 us
    all_gather x1, waiting for transfers between devices, shards(): states = lax.all_gather(state.astype(jnp.bfloat16), 'seq')  80.2 us
    ppermute x1, waiting for transfers between devices, shards(): lax.ppermute(piece, 'head', [(i, (i + shift) % halves) for i in range(hal...  24.1 us
    dot_general x2, matrix products, feature_map(): proj = jnp.einsum('htd,hdm->htm', x, direction, precision=HIGH)  11.9 us
    reduce_sum x1, other arithmetic, shards(): prior = jnp.sum(jnp.where(earlier, states.astype(jnp.float32), 0.0), axis=0)  11.7 us
    dot_general x1, matrix products, shards(): partial = jnp.dot(attended, whole, preferred_element_type=jnp.float32)  8.28 us
    dot_general x1, matrix products, shards(): scores = jnp.einsum('htm,hsm->hts', qf, kf, precision=HIGH) * lower  6.97 us
  transfers between devices with their start and end apart: 3, of which 3 were waited for; matrix products, arithmetic and copies ran while one was open for 11% of the time, Pallas kernels for 0%

commit v1 on v0

--- a/solution.py
+++ b/solution.py
@@ -7,6 +7,18 @@
 DH = 128
 M = 256
 HIGH = lax.Precision.HIGHEST
+
+
+def doubled_up(shard, axis, dim):
+    ways, here = (lax.axis_size(axis), lax.axis_index(axis))
+    grown, reach = (shard, 1)
+    while reach < ways:
+        theirs = lax.ppermute(grown, axis, [(d, d ^ reach) for d in range(ways)])
+        mine_first = jnp.concatenate([grown, theirs], axis=dim)
+        theirs_first = jnp.concatenate([theirs, grown], axis=dim)
+        grown = jnp.where(here & reach == 0, mine_first, theirs_first)
+        reach = 2 * reach
+    return grown
 
 
 def feature_map(x, direction):
@@ -30,7 +42,7 @@
     state = jnp.einsum("htp,htk->hpk", v, kf, precision=HIGH)
     states = lax.all_gather(state.astype(jnp.bfloat16), "seq")
     state, weight = lax.optimization_barrier((state, output_proj_weight))
-    whole = lax.all_gather(weight, "seq", axis=1, tiled=True)
+    whole = doubled_up(weight, "seq", 1)
     qf = feature_map(split_heads(queries), features)
     lower = jnp.tril(jnp.ones((tok_rows, tok_rows), jnp.float32))
     scores = jnp.einsum("htm,hsm->hts", qf, kf, precision=HIGH) * lower

time: 299 us -> 674 us (2.25)
  waiting for transfers between devices: 217 us -> 555 us
  other arithmetic: 18.8 us -> 40.8 us
  matrix products: 40.9 us -> 48.4 us
  starting transfers between devices: 1.52 us -> 9.02 us
    ppermute x0 -> x4, waiting for transfers between devices: none -> 532 us  [doubled_up(): theirs = lax.ppermute(grown, axis, [(d, d ^ reach) for d in range(ways)])]
    all_gather x1 -> x0, waiting for transfers between devices: 112 us -> none  [shards(): whole = lax.all_gather(weight, 'seq', axis=1, tiled=True)]
    all_gather x1, waiting for transfers between devices: 80.2 us -> 0.01 us  [shards(): states = lax.all_gather(state.astype(jnp.bfloat16), 'seq')]
    select_n x0 -> x3, other arithmetic: none -> 22 us  [doubled_up(): grown = jnp.where(here & reach == 0, mine_first, theirs_first)]
    ppermute x0 -> x4, starting transfers between devices: none -> 7.57 us  [doubled_up(): theirs = lax.ppermute(grown, axis, [(d, d ^ reach) for d in range(ways)])]
    dot_general x1, matrix products: 8.28 us -> 15.8 us  [shards(): partial = jnp.dot(attended, whole, preferred_element_type=jnp.float32)]
  transfers between devices with their start and end apart: 3 -> 6, of which waited for: 3 -> 5; matrix products, arithmetic and copies ran while one was open for 11% -> 8% of each run, Pallas kernels for 0% -> 0%
where the time goes in v1:
time: 674 us; the launch traced here: 673 us
  waiting for transfers between devices  555 us (82%)
  matrix products  48.4 us (7%)
  other arithmetic  40.8 us (6%)
  between operations  13.6 us (2%)
  starting transfers between devices  9.02 us (1%)
    ppermute x4, waiting for transfers between devices, doubled_up(): theirs = lax.ppermute(grown, axis, [(d, d ^ reach) for d in range(ways)])  532 us
    ppermute x1, waiting for transfers between devices, shards(): lax.ppermute(piece, 'head', [(i, (i + shift) % halves) for i in range(hal...  23.2 us
    select_n x3, other arithmetic, doubled_up(): grown = jnp.where(here & reach == 0, mine_first, theirs_first)  22 us
    dot_general x1, matrix products, shards(): partial = jnp.dot(attended, whole, preferred_element_type=jnp.float32)  15.8 us
  transfers between devices with their start and end apart: 6, of which 5 were waited for; matrix products, arithmetic and copies ran while one was open for 8% of the time, Pallas kernels for 0%

profile of v1, /device:TPU:0, one launch (start us, length us, event | category | flops | bytes accessed | tf_op | source)
XLA Modules:
  0.0 673.5 jit_solution(7712596965594915769)
XLA Ops:
  6.5 0.0 copy-start
  6.5 0.0 all-gather.3.cloned.1.call-start
  6.5 2.0 fusion.15
  8.5 0.0 copy-done
  8.5 6.9 %fusion.14 = f32[16,256,256]{2,1,0:T(8,128)} fusion(f32[16,128,256]{2,1,0:T(8,128)S(1)} %copy-done, bf16[256,2048]{1,0:T(8,128)(2,1)} %param.6), kind=kOutput, calls=%fused_computation.21 | convolution fusion | flops 1611661312 | bytes 7340032 | tf_op jit(solution)/shard_map/htd,hdm->htm/dot_general | solution.py:26
  15.5 1.5 copy.11
  17.0 5.6 fusion.12
  22.6 0.0 all-gather.3.cloned.1.call-update
  22.6 0.5 collective-permute-start
  23.1 2.6 collective-permute-done
  25.7 4.1 maximum_select_fusion.4
  29.9 2.9 collective-permute-start.1
  32.7 91.2 %collective-permute-done.1 = bf16[2048,512]{1,0:T(8,128)(2,1)} collective-permute-done((bf16[2048,512]{1,0:T(8,128)(2,1)}, bf16[2048,512]{1,0:T(8,128)(2,1)}, u32[]{:S(2)}, u32[]{:S(2)}) %collective-permute-start.1) | collective-permute-done | bytes 2097184 | tf_op jit(solution)/shard_map/ppermute | solution.py:16
  123.9 6.6 maximum_select_fusion.3
  130.5 0.0 collective-permute-start.2
  130.5 113.8 %collective-permute-done.2 = bf16[2048,1024]{1,0:T(8,128)(2,1)} collective-permute-done((bf16[2048,1024]{1,0:T(8,128)(2,1)}, bf16[2048,1024]{1,0:T(8,128)(2,1)}, u32[]{:S(2)}, u32[]{:S(2)}) %collective-permute-start.2) | collective-permute-done | bytes 4194336 | tf_op jit(solution)/shard_map/ppermute | solution.py:16
  244.3 11.3 %maximum_select_fusion.2 = bf16[2048,2048]{1,0:T(8,128)(2,1)} fusion(bf16[2048,1024]{1,0:T(8,128)(2,1)} %collective-permute-done.2, bf16[2048,1024]{1,0:T(8,128)(2,1)} %maximum_select_fusion.3, pred[]{:T(512)S(6)} %eq.13), kind=kLoop, calls=%fused_computation.10 | loop fusion | flops 37748736 | bytes 16777216 | tf_op jit(solution)/shard_map/jit(_where)/select_n | solution.py:19
  255.7 4.2 collective-permute-start.3
  259.9 0.0 copy-start.2
  259.9 2.0 fusion.18
  261.9 4.9 fusion.17
  266.8 0.0 copy-start.3
  266.8 2.0 copy-done.3
  268.8 0.0 copy-done.2
  268.8 7.0 %fusion.11 = f32[16,256,256]{2,1,0:T(8,128)} fusion(f32[16,256,256]{2,1,0:T(8,128)S(1)} %fusion.17, f32[16,256,256]{2,1,0:T(8,128)S(1)} %copy-done.2, f32[16,256]{1,0:T(8,128)S(1)} %broadcast_multiply_fusion, f32[16,256]{1,0:T(8,128)S(1)} %broadcast_multiply_fusion.1), kind=kOutput, calls=%fused_computation.17 | convolution fusion | flops 3225419776 | bytes 12615680 | tf_op jit(solution)/shard_map/htm,hsm->hts/dot_general | solution.py:48
  275.8 0.0 all-gather.3.cloned.1.call-done
  275.8 0.0 copy-start.4
  275.8 11.6 %fusion = f32[16,136,256]{2,1,0:T(8,128)S(1)} fusion(bf16[16,16,136,256]{3,2,1,0:T(8,128)(2,1)} %bitcast.53, pred[16]{0:T(512)(128)(4,1)S(1)} %iota_compare_fusion.1), kind=kLoop, calls=%fused_computation.1 | loop fusion | flops 26181632 | bytes 20054032 | tf_op jit(solution)/shard_map/reduce_sum | solution.py:51
  287.4 0.0 copy-done.4
  287.4 0.0 copy-start.5
  287.4 5.5 fusion.10
  292.9 0.0 copy-done.5
  292.9 2.7 fusion.30
  295.7 0.2 fusion.19
  295.9 324.3 %collective-permute-done.3 = bf16[2048,2048]{1,0:T(8,128)(2,1)} collective-permute-done((bf16[2048,2048]{1,0:T(8,128)(2,1)}, bf16[2048,2048]{1,0:T(8,128)(2,1)}, u32[]{:S(2)}, u32[]{:S(2)}) %collective-permute-start.3) | collective-permute-done | bytes 8388640 | tf_op jit(solution)/shard_map/ppermute | solution.py:16
  620.2 0.0 copy-start.1
  620.2 15.8 %fusion.1 = f32[256,4096]{1,0:T(8,128)S(1)} fusion(bf16[256,2048]{0,1:T(8,128)(2,1)S(1)} %bitcast.56, bf16[2048,2048]{1,0:T(8,128)(2,1)} %collective-permute-done.3, bf16[2048,2048]{1,0:T(8,128)(2,1)} %maximum_select_fusion.2, pred[]{:T(512)S(6)} %eq.12), kind=kOutput, calls=%fused_computation.3 | convolution fusion | flops 4370464768 | bytes 22020096 | tf_op jit(solution)/shard_map/dot_general | solution.py:55
  636.0 0.0 copy-start.6
  636.0 1.9 copy-done.6
  638.0 1.1 dynamic-slice_convert_fusion
  639.1 1.5 collective-permute-start.4
  640.5 23.2 %collective-permute-done.4 = bf16[256,2048]{1,0:T(8,128)(2,1)S(1)} collective-permute-done((bf16[256,2048]{1,0:T(8,128)(2,1)}, bf16[256,2048]{1,0:T(8,128)(2,1)S(1)}, u32[]{:S(2)}, u32[]{:S(2)}) %collective-permute-start.4) | collective-permute-done | bytes 1048608 | tf_op jit(solution)/shard_map/ppermute | solution.py:61
  663.8 2.9 add_convert_fusion
  666.6 0.0 copy-done.1
  (6 shorter events, 0.0 us)
Async XLA Ops:
  6.5 2.0 copy-start
  6.5 269.2 %all-gather.3.cloned.1.call-start = ((), (), s32[]{:S(2)}) async-start(), calls=%async_computation | async-start | bytes 18939904 | tf_op jit(solution)/shard_map/all_gather | solution.py:43
  22.6 3.1 collective-permute-start
  29.9 94.1 %collective-permute-start.1 = (bf16[2048,512]{1,0:T(8,128)(2,1)}, bf16[2048,512]{1,0:T(8,128)(2,1)}, u32[]{:S(2)}, u32[]{:S(2)}) collective-permute-start(bf16[2048,512]{1,0:T(8,128)(2,1)} %maximum_select_fusion.4), channel_id=1, source_target_pairs={{0,4},{2,6},{4,0},{6,2},{8,12},{10,14},{12,8},{14,10},{16,20},{18,... | collective-permute-start | bytes 6291464 | tf_op jit(solution)/shard_map/ppermute | solution.py:16
  130.5 113.8 %collective-permute-start.2 = (bf16[2048,1024]{1,0:T(8,128)(2,1)}, bf16[2048,1024]{1,0:T(8,128)(2,1)}, u32[]{:S(2)}, u32[]{:S(2)}) collective-permute-start(bf16[2048,1024]{1,0:T(8,128)(2,1)} %maximum_select_fusion.3), channel_id=1, source_target_pairs={{0,8},{2,10},{4,12},{6,14},{8,0},{10,2},{12,4},{14,6},{16,24},{18,... | collective-permute-start | bytes 12582920 | tf_op jit(solution)/shard_map/ppermute | solution.py:16
  255.7 364.6 %collective-permute-start.3 = (bf16[2048,2048]{1,0:T(8,128)(2,1)}, bf16[2048,2048]{1,0:T(8,128)(2,1)}, u32[]{:S(2)}, u32[]{:S(2)}) collective-permute-start(bf16[2048,2048]{1,0:T(8,128)(2,1)} %maximum_select_fusion.2), channel_id=1, source_target_pairs={{0,16},{2,18},{4,20},{6,22},{8,24},{10,26},{12,28},{14,30},{16,0},... | collective-permute-start | bytes 25165832 | tf_op jit(solution)/shard_map/ppermute | solution.py:16
  259.9 8.9 %copy-start.2 = (f32[16,256,256]{2,1,0:T(8,128)S(1)}, f32[16,256,256]{2,1,0:T(8,128)}, u32[]{:S(2)}) copy-start(f32[16,256,256]{2,1,0:T(8,128)} %fusion.14) | copy-start | bytes 12582916
  266.8 2.0 copy-start.3
  275.8 11.7 %copy-start.4 = (f32[16,256,256]{2,1,0:T(8,128)S(1)}, f32[16,256,256]{2,1,0:T(8,128)}, u32[]{:S(2)}) copy-start(f32[16,256,256]{2,1,0:T(8,128)} %copy-done.3) | copy-start | bytes 12582916
  287.4 5.5 copy-start.5
  620.2 46.4 %copy-start.1 = (f32[16,128,256]{2,1,0:T(8,128)S(1)}, f32[16,128,256]{2,1,0:T(8,128)}, u32[]{:S(2)}) copy-start(f32[16,128,256]{2,1,0:T(8,128)} %param.8) | copy-start | bytes 6291460
  636.0 1.9 copy-start.6
  639.1 24.7 %collective-permute-start.4 = (bf16[256,2048]{1,0:T(8,128)(2,1)}, bf16[256,2048]{1,0:T(8,128)(2,1)S(1)}, u32[]{:S(2)}, u32[]{:S(2)}) collective-permute-start(bf16[256,2048]{1,0:T(8,128)(2,1)} %dynamic-slice_convert_fusion), channel_id=1, source_target_pairs={{0,1},{1,0},{2,3},{3,2},{4,5},{5,4},{6,7},{7,6},{8,9},{9,8},{10,11... | collective-permute-start | bytes 3145736 | tf_op jit(solution)/shard_map/ppermute | solution.py:61
Sparse Core Ops, SparseCore 0:
  22.7 155.4 all-gather.2
